TPU v7x, 32 devices: a whole 2x2x4 slice. The times are simulated.
32 devices in a mesh: row: 4 (over z), col: 8 (over y, x, core).
Axes of the slice: x: 2, y: 2, z: 4, core: 2. Of those that a mesh axis runs over, the one named last changes fastest.
Arguments:
- occupations: int32 [4096, 128], P('row'), may hold values from 0 to 2
- table: float32 [384, 1024], replicated, may hold values from -0.5 to 0.5
- weights: float32 [2, 1024, 4096], P(None, None, 'col'), may hold values from -0.1875 to 0.1875
- biases: float32 [2, 4096], P(None, 'col'), may hold values from -6 to 6
- heads: float32 [2, 4096], P(None, 'col'), may hold values from -18 to 18
- energies: float32 [4096], P('row'), may hold values from -6 to 6
Outputs:
- schur: float32 [4096, 4096], P('row', 'col')
- solved_rhs: float32 [4096], P('row')
All inputs are finite; a program needn't handle non-finite values.
Results may differ from a plain program's by a relative error of at most 0.0034.
Values may be sent and summed in bfloat16 or wider, within the bound.
A program may use at most 128 MiB of HBM per device.

v0:
```python
import math
import jax
import jax.numpy as jnp
from jax import lax
from jax.sharding import PartitionSpec as P

norm_eps = 1e-06
diag_shift = 0.05


def broadcast(block, axis, holder):
    block = jnp.where(lax.axis_index(axis) == holder, block, jnp.zeros_like(block))
    return lax.psum(block, axis)


def jacobian(occupations, table, weights, biases, heads):
    onehot = jnp.concatenate(
        [
            (occupations == 0).astype(jnp.float32),
            (occupations == 1).astype(jnp.float32),
            (occupations == 2).astype(jnp.float32),
        ],
        axis=1,
    )
    embedded = jnp.dot(
        onehot, table, precision=lax.Precision.HIGHEST, preferred_element_type=jnp.float32
    )
    embedded = embedded * lax.rsqrt(
        jnp.mean(embedded * embedded, axis=-1, keepdims=True) + norm_eps
    )
    blocks = []
    for panel_index in range(2):
        hidden = (
            jnp.dot(
                embedded,
                weights[panel_index],
                precision=lax.Precision.HIGHEST,
                preferred_element_type=jnp.float32,
            )
            + biases[panel_index]
        )
        blocks.append(heads[panel_index] * jax.nn.sigmoid(hidden))
    return jnp.concatenate(blocks, axis=1)


def on_device(occupations, table, weights, biases, heads, energies):
    row_count = occupations.shape[0]
    row_devices = lax.axis_size("row")
    col_devices = lax.axis_size("col")
    sample_total = row_count * row_devices
    panel_width = sample_total // col_devices
    derivs = jacobian(occupations, table, weights, biases, heads)
    col_sums = lax.psum(jnp.sum(derivs, axis=0), "row")
    centered = ((derivs - col_sums / sample_total) * (1.0 / math.sqrt(sample_total))).astype(
        jnp.bfloat16
    )
    own_rows = lax.all_gather(centered, "col", axis=1, tiled=True)
    every_sample = lax.all_gather(centered, "row", axis=0, tiled=True)
    partner = lax.all_to_all(every_sample, "col", split_axis=0, concat_axis=1, tiled=True)
    kernel = lax.dot_general(
        own_rows, partner, (((1,), (1,)), ((), ())), preferred_element_type=jnp.float32
    )
    row_ids = lax.axis_index("row") * row_count + lax.iota(jnp.int32, row_count)
    col_ids = lax.axis_index("col") * panel_width + lax.iota(jnp.int32, panel_width)
    kernel = kernel + jnp.where(row_ids[:, None] == col_ids[None, :], diag_shift, 0.0).astype(
        jnp.float32
    )
    right_side = energies
    for panel_index in range(2):
        start_global = panel_index * panel_width
        root_row = start_global // row_count
        offset = start_global % row_count
        top_block, top_side = (
            broadcast(kernel[offset : offset + panel_width], "row", root_row),
            broadcast(right_side[offset : offset + panel_width], "row", root_row),
        )
        column, diag_block = (
            broadcast(kernel, "col", panel_index),
            broadcast(top_block, "col", panel_index),
        )
        factor = jnp.linalg.cholesky(diag_block)
        left_rows = lax.linalg.triangular_solve(
            factor, column, left_side=False, lower=True, transpose_a=True
        )
        right_rows = lax.linalg.triangular_solve(
            factor, top_block.T, left_side=False, lower=True, transpose_a=True
        )
        kernel = kernel - lax.dot_general(
            left_rows,
            right_rows,
            (((1,), (1,)), ((), ())),
            precision=lax.Precision.HIGHEST,
            preferred_element_type=jnp.float32,
        )
        solved = lax.linalg.triangular_solve(factor, top_side[:, None], left_side=True, lower=True)[
            :, 0
        ]
        right_side = right_side - jnp.dot(
            left_rows, solved, precision=lax.Precision.HIGHEST, preferred_element_type=jnp.float32
        )
        placed = right_side.at[offset : offset + panel_width].set(solved)
        right_side = jnp.where(lax.axis_index("row") == root_row, placed, right_side)
    return (kernel, right_side)


def solution(mesh):
    placed = (P("row", None), P(), P(None, None, "col"), P(None, "col"), P(None, "col"), P("row"))
    return jax.shard_map(
        on_device,
        mesh=mesh,
        in_specs=placed,
        out_specs=(P("row", "col"), P("row")),
        check_vma=False,
    )
```

profile of v0, /device:TPU:0, one launch (start us, length us, event | category | flops | bytes accessed | tf_op | source)
XLA Modules:
  0.0 969.1 jit_solution(3831402307478594253)
XLA Ops:
  13.9 12.5 %divide_multiply_fusion.1 = f32[1024,512]{0,1:T(8,128)S(1)} fusion(f32[2,1024,512]{2,1,0:T(8,128)} %param.19, f32[1024,1024]{0,1:T(8,128)} %get-tuple-element.136, f32[1024]{0:T(1024)S(1)} %add_rsqrt_fusion, f32[512]{0:T(512)S(1)} %bitcast.291, f32[512]{0:T(512)S(1)} %bitcast.290), kind=kOutput, calls=%fused_computation.20 | convolution fusion | flops 6446120960 | bytes 8396800 | tf_op jit(solution)/shard_map/dot_general | solution.py:34
  26.4 7.2 divide_multiply_fusion
  35.6 13.7 %all-reduce.3 = (f32[1024]{0:T(1024)S(1)}, f32[512,1]{0,1:T(1,128)S(1)}) all-reduce(f32[1024]{0:T(1024)S(1)} %fusion.4, f32[512,1]{0,1:T(1,128)S(1)} %bitcast.282), channel_id=1, replica_groups=mesh['row'=4,'col'=8] {'row'}, use_global_device_ids=true, to_apply=%region_2.0 | all-reduce | flops 1536 | bytes 12288 | tf_op jit(solution)/shard_map/psum | solution.py:53
  54.1 147.2 %all-gather.5.cloned.1.call-done = bf16[4096,1024]{0,1:T(8,128)(2,1)} async-done(((bf16[1024,1024]{0,1:T(8,128)(2,1)}), bf16[4096,1024]{0,1:T(8,128)(2,1)}) %all-gather.5.cloned.1.call-update) | async-done | bytes 8388624 | tf_op jit(solution)/shard_map/all_gather | solution.py:58
  201.3 7.9 copy.26
  214.2 126.8 %all-to-all-done = bf16[8,512,1024]{1,2,0:T(8,128)(2,1)} async-done(((bf16[8,512,1024]{1,2,0:T(8,128)(2,1)}), bf16[8,512,1024]{1,2,0:T(8,128)(2,1)}, u32[]{:S(2)}, u32[]{:S(2)}) %all-to-all-start) | async-done | bytes 8388640 | tf_op jit(solution)/shard_map/all_to_all | solution.py:59
  341.0 32.8 %all-gather.3.cloned.1.call-done = bf16[1024,8192]{0,1:T(8,128)(2,1)} async-done(((bf16[1024,1024]{0,1:T(8,128)(2,1)}), bf16[1024,8192]{0,1:T(8,128)(2,1)}) %all-gather.3.cloned.1.call-update) | async-done | bytes 16777232 | tf_op jit(solution)/shard_map/all_gather | solution.py:57
  373.8 15.9 %broadcast_select_fusion.1 = (f32[1024,512]{0,1:T(8,128)}, f32[1024,512]{0,1:T(8,128)S(1)}) fusion(pred[]{:T(512)S(6)} %eq.56, s32[512]{0:T(512)S(1)} %iota_add_fusion.1, s32[1024]{0:T(1024)S(1)} %iota_add_fusion, bf16[1024,8192]{0,1:T(8,128)(2,1)} %all-gather.3.cloned.1.call-done, bf16[512,8192]{0,1:T(8,128)(2,1)} %bitcast.7), kind=kOutput, calls=%fused_computation.118 | convolution fusion | flops 8592031744 | bytes 29366272 | tf_op jit(solution)/shard_map/dot_general | solution.py:60
  392.2 51.6 %all-reduce.9.cloned.1.call-done = f32[512,512]{0,1:T(8,128)} async-done(((f32[512,512]{0,1:T(8,128)}), f32[512,512]{0,1:T(8,128)}) %all-reduce.9.cloned.1.call-update) | async-done | bytes 1048592 | tf_op jit(solution)/shard_map/psum | solution.py:13
  446.6 69.6 %all-reduce.15.cloned.1.call-done = (f32[1024,512]{0,1:T(8,128)}, f32[512,512]{0,1:T(8,128)}) async-done(((f32[1024,512]{0,1:T(8,128)}, f32[512,512]{0,1:T(8,128)}), (f32[1024,512]{0,1:T(8,128)}, f32[512,512]{0,1:T(8,128)})) %all-reduce.15.cloned.1.call-update) | async-done | bytes 3145744 | tf_op jit(solution)/shard_map/psum | solution.py:13
  519.1 11.7 %cholesky.286 = f32[128,128]{1,0:T(8,128)S(1)} custom-call(f32[128,128]{1,0:T(8,128)S(1)} %cholesky.426), custom_call_target="Cholesky" | custom-call | tf_op jit(solution)/shard_map/jit(cholesky)/cholesky | solution.py:81
  531.0 9.8 %custom-call.35 = f32[1,128,128]{1,2,0:T(8,128)S(1)} custom-call(f32[1,128,128]{2,1,0:T(8,128)S(1)} %get-tuple-element.130), custom_call_target="InvertDiagBlocksLowerTriangular" | custom-call | tf_op jit(solution)/shard_map/jit(cholesky)/cholesky | solution.py:81
  543.3 11.7 %cholesky.305 = f32[128,128]{1,0:T(8,128)S(1)} custom-call(f32[128,128]{1,0:T(8,128)S(1)} %cholesky.430), custom_call_target="Cholesky" | custom-call | tf_op jit(solution)/shard_map/jit(cholesky)/cholesky | solution.py:81
  555.1 10.0 %custom-call.36 = f32[1,128,128]{1,2,0:T(8,128)S(1)} custom-call(f32[1,128,128]{2,1,0:T(8,128)S(1)} %get-tuple-element.127), custom_call_target="InvertDiagBlocksLowerTriangular" | custom-call | tf_op jit(solution)/shard_map/jit(cholesky)/cholesky | solution.py:81
  566.6 11.7 %cholesky.326 = f32[128,128]{1,0:T(8,128)S(1)} custom-call(f32[128,128]{1,0:T(8,128)S(1)} %cholesky.435), custom_call_target="Cholesky" | custom-call | tf_op jit(solution)/shard_map/jit(cholesky)/cholesky | solution.py:81
  579.0 9.8 %custom-call.37 = f32[1,128,128]{1,2,0:T(8,128)S(1)} custom-call(f32[1,128,128]{2,1,0:T(8,128)S(1)} %get-tuple-element.124), custom_call_target="InvertDiagBlocksLowerTriangular" | custom-call | tf_op jit(solution)/shard_map/jit(cholesky)/cholesky | solution.py:81
  590.3 11.7 %cholesky.343 = f32[128,128]{1,0:T(8,128)S(1)} custom-call(f32[128,128]{1,0:T(8,128)S(1)} %convolution_subtract_fusion.17), custom_call_target="Cholesky" | custom-call | tf_op jit(solution)/shard_map/jit(cholesky)/cholesky | solution.py:81
  606.6 8.0 while.14
  614.7 39.3 %custom-call.38 = f32[4,128,128]{1,2,0:T(8,128)S(1)} custom-call(f32[4,128,128]{2,1,0:T(8,128)S(1)} %get-tuple-element.72), custom_call_target="InvertDiagBlocksLowerTriangular" | custom-call | tf_op jit(solution)/shard_map/triangular_solve/custom-call.3 | solution.py:82
  676.3 51.5 %all-reduce.11.cloned.1.call-done = f32[512,512]{0,1:T(8,128)} async-done(((f32[512,512]{0,1:T(8,128)}), f32[512,512]{0,1:T(8,128)}) %all-reduce.11.cloned.1.call-update) | async-done | bytes 1048592 | tf_op jit(solution)/shard_map/psum | solution.py:13
  731.1 10.1 %psum.71 = f32[512,1]{0,1:T(1,128)S(1)} all-reduce(f32[512,1]{0,1:T(1,128)S(1)} %bitcast.285), channel_id=1, replica_groups=mesh['row'=4,'col'=8] {'row'}, use_global_device_ids=true, to_apply=%region_18.23 | all-reduce | flops 512 | bytes 4096 | tf_op jit(solution)/shard_map/psum | solution.py:13
  741.3 58.9 %all-reduce.13.cloned.1.call-done = (f32[1024,512]{0,1:T(8,128)}, f32[512,512]{0,1:T(8,128)}) async-done(((f32[1024,512]{0,1:T(8,128)}, f32[512,512]{0,1:T(8,128)}), (f32[1024,512]{0,1:T(8,128)}, f32[512,512]{0,1:T(8,128)})) %all-reduce.13.cloned.1.call-update) | async-done | bytes 3145744 | tf_op jit(solution)/shard_map/psum | solution.py:13
  803.1 11.7 %cholesky.358 = f32[128,128]{1,0:T(8,128)S(1)} custom-call(f32[128,128]{1,0:T(8,128)S(1)} %cholesky.439), custom_call_target="Cholesky" | custom-call | tf_op jit(solution)/shard_map/jit(cholesky)/cholesky | solution.py:81
  815.0 9.8 %custom-call.40 = f32[1,128,128]{1,2,0:T(8,128)S(1)} custom-call(f32[1,128,128]{2,1,0:T(8,128)S(1)} %get-tuple-element.120), custom_call_target="InvertDiagBlocksLowerTriangular" | custom-call | tf_op jit(solution)/shard_map/jit(cholesky)/cholesky | solution.py:81
  827.3 11.7 %cholesky.377 = f32[128,128]{1,0:T(8,128)S(1)} custom-call(f32[128,128]{1,0:T(8,128)S(1)} %cholesky.443), custom_call_target="Cholesky" | custom-call | tf_op jit(solution)/shard_map/jit(cholesky)/cholesky | solution.py:81
  840.4 10.2 %custom-call.41 = f32[1,128,128]{1,2,0:T(8,128)S(1)} custom-call(f32[1,128,128]{2,1,0:T(8,128)S(1)} %get-tuple-element.117), custom_call_target="InvertDiagBlocksLowerTriangular" | custom-call | tf_op jit(solution)/shard_map/jit(cholesky)/cholesky | solution.py:81
  852.2 11.7 %cholesky.398 = f32[128,128]{1,0:T(8,128)S(1)} custom-call(f32[128,128]{1,0:T(8,128)S(1)} %cholesky.448), custom_call_target="Cholesky" | custom-call | tf_op jit(solution)/shard_map/jit(cholesky)/cholesky | solution.py:81
  864.7 9.8 %custom-call.42 = f32[1,128,128]{1,2,0:T(8,128)S(1)} custom-call(f32[1,128,128]{2,1,0:T(8,128)S(1)} %get-tuple-element.114), custom_call_target="InvertDiagBlocksLowerTriangular" | custom-call | tf_op jit(solution)/shard_map/jit(cholesky)/cholesky | solution.py:81
  875.9 11.7 %cholesky.415 = f32[128,128]{1,0:T(8,128)S(1)} custom-call(f32[128,128]{1,0:T(8,128)S(1)} %convolution_subtract_fusion.16), custom_call_target="Cholesky" | custom-call | tf_op jit(solution)/shard_map/jit(cholesky)/cholesky | solution.py:81
  891.3 8.0 while.15
  899.3 39.3 %custom-call.43 = f32[4,128,128]{1,2,0:T(8,128)S(1)} custom-call(f32[4,128,128]{2,1,0:T(8,128)S(1)} %get-tuple-element.74), custom_call_target="InvertDiagBlocksLowerTriangular" | custom-call | tf_op jit(solution)/shard_map/triangular_solve/custom-call.3 | solution.py:82
  953.3 5.2 convolution_subtract_fusion
  (196 shorter events, 105.8 us)
Async XLA Ops:
  7.2 1.6 copy-start
  7.2 194.1 %all-gather.5.cloned.1.call-start = ((), (), s32[]{:S(2)}) async-start(), calls=%async_computation.2 | async-start | bytes 10485760 | tf_op jit(solution)/shard_map/all_gather | solution.py:58
  8.7 5.1 copy-start.19
  8.7 5.1 copy-start.20
  13.8 12.6 %copy-start.21 = (f32[2,1024,512]{2,1,0:T(8,128)S(1)}, f32[2,1024,512]{2,1,0:T(8,128)}, u32[]{:S(2)}) copy-start(f32[2,1024,512]{2,1,0:T(8,128)} %param.19) | copy-start | bytes 12582916
  13.9 12.6 %copy-start.22 = (f32[1024,1024]{0,1:T(8,128)S(1)}, f32[1024,1024]{0,1:T(8,128)}, u32[]{:S(2)}) copy-start(f32[1024,1024]{0,1:T(8,128)} %get-tuple-element.136) | copy-start | bytes 12582916
  26.4 7.2 copy-start.4
  33.6 1.3 copy-start.5
  34.9 0.7 copy-start.17
  53.3 320.5 %all-gather.3.cloned.1.call-start = ((), (), s32[]{:S(2)}) async-start(), calls=%async_computation.1 | async-start | bytes 18874368 | tf_op jit(solution)/shard_map/all_gather | solution.py:57
  209.1 131.9 %all-to-all-start = ((bf16[8,512,1024]{1,2,0:T(8,128)(2,1)}), bf16[8,512,1024]{1,2,0:T(8,128)(2,1)}, u32[]{:S(2)}, u32[]{:S(2)}) async-start(bf16[8,512,1024]{1,2,0:T(8,128)(2,1)} %bitcast.258), calls=%async_computation | async-start | bytes 16777216 | tf_op jit(solution)/shard_map/all_to_all | solution.py:59
  214.1 229.6 %all-reduce.9.cloned.1.call-start = ((), (), s32[]{:S(2)}) async-start(), calls=%async_computation.3 | async-start | bytes 2097152 | tf_op jit(solution)/shard_map/psum | solution.py:13
  389.7 1.4 copy-start.6
  392.2 124.1 %all-reduce.15.cloned.1.call-start = ((), (), s32[]{:S(2)}) async-start(), calls=%async_computation.6 | async-start | bytes 6291456 | tf_op jit(solution)/shard_map/psum | solution.py:13
  446.1 281.7 %all-reduce.11.cloned.1.call-start = ((), (), s32[]{:S(2)}) async-start(), calls=%async_computation.4 | async-start | bytes 2097152 | tf_op jit(solution)/shard_map/psum | solution.py:13
  516.2 1.7 copy-start.9
  518.1 1.0 copy-start.13
  660.3 2.9 copy-start.11
  663.3 4.8 copy-start.14
  664.3 3.7 copy-start.7
  673.2 1.4 copy-start.2
  675.7 124.5 %all-reduce.13.cloned.1.call-start = ((), (), s32[]{:S(2)}) async-start(), calls=%async_computation.5 | async-start | bytes 6291456 | tf_op jit(solution)/shard_map/psum | solution.py:13
  728.9 1.0 copy-start.15
  800.2 1.7 copy-start.8
  802.1 1.0 copy-start.12
  939.4 4.7 copy-start.16
  946.6 1.8 copy-start.10
  949.5 3.8 copy-start.3
  953.3 8.7 copy-start.1
  961.4 0.6 copy-start.18
Sparse Core Ops, SparseCore 0:
  53.5 147.7 all-gather.4
  203.1 170.6 all-gather.2
  392.3 51.4 all-reduce.8
  447.6 68.6 all-reduce.14
  675.8 51.9 all-reduce.10
  731.6 68.6 all-reduce.12
where the time goes:
time: 975 us; the launch traced here: 969 us
  waiting for transfers between devices  539 us (55%)
  other arithmetic  249 us (26%)
  matrix products  92.9 us (10%)
  local copies, waits for them, and re-layouts  37.6 us (4%)
  blocking collectives  23.8 us (2%)
  between operations  20.4 us (2%)
    psum x4, waiting for transfers between devices, broadcast(): return lax.psum(block, axis)  232 us
    another operation x29, other arithmetic, on_device(): factor = jnp.linalg.cholesky(diag_block)  158 us
    all_gather x1, waiting for transfers between devices, on_device(): every_sample = lax.all_gather(centered, 'row', axis=0, tiled=True)  147 us
    all_to_all x1, waiting for transfers between devices, on_device(): lax.all_to_all(every_sample, 'col', split_axis=0, concat_axis=1, tiled=True)  127 us
    another operation x5, other arithmetic, on_device(): lax.linalg.triangular_solve(factor, column, left_side=False, lower=True,...  79.4 us
    all_gather x1, waiting for transfers between devices, on_device(): own_rows = lax.all_gather(centered, 'col', axis=1, tiled=True)  32.8 us
    dot_general x2, matrix products, jacobian(): jnp.dot(embedded, weights[panel_index], precision=lax.Precision.HIGHEST,...  19.7 us
  transfers between devices with their start and end apart: 7, of which 7 were waited for; matrix products, arithmetic and copies ran while one was open for 1% of the time, Pallas kernels for 0%

commit v1 on v0

--- a/solution.py
+++ b/solution.py
@@ -10,7 +10,7 @@
 
 def broadcast(block, axis, holder):
     block = jnp.where(lax.axis_index(axis) == holder, block, jnp.zeros_like(block))
-    return lax.psum(block, axis)
+    return jnp.sum(lax.all_gather(block, axis), axis=0)
 
 
 def jacobian(occupations, table, weights, biases, heads):

time: 975 us -> 1040 us (1.067)
  other arithmetic: 249 us -> 285 us
  blocking collectives: 23.8 us -> 37.8 us
    all_gather x0 -> x6, waiting for transfers between devices: none -> 237 us  [broadcast(): return jnp.sum(lax.all_gather(block, axis), axis=0)]
    psum x4 -> x0, waiting for transfers between devices: 232 us -> none  [broadcast(): return lax.psum(block, axis)]
    reduce_sum x0 -> x8, other arithmetic: none -> 33.4 us  [broadcast(): return jnp.sum(lax.all_gather(block, axis), axis=0)]
    all_gather x0 -> x2, blocking collectives: none -> 24.3 us  [broadcast(): return jnp.sum(lax.all_gather(block, axis), axis=0)]
  transfers between devices with their start and end apart: 7 -> 9, of which waited for: 7 -> 7; matrix products, arithmetic and copies ran while one was open for 1% -> 30% of each run, Pallas kernels for 0% -> 0%
where the time goes in v1:
time: 1040 us; the launch traced here: 1030 us
  waiting for transfers between devices  546 us (52%)
  other arithmetic  285 us (27%)
  matrix products  95.1 us (9%)
  local copies, waits for them, and re-layouts  40.8 us (4%)
  blocking collectives  37.8 us (4%)
  between operations  20.2 us (2%)
    all_gather x6, waiting for transfers between devices, broadcast(): return jnp.sum(lax.all_gather(block, axis), axis=0)  237 us
    another operation x29, other arithmetic, on_device(): factor = jnp.linalg.cholesky(diag_block)  158 us
    all_gather x1, waiting for transfers between devices, on_device(): every_sample = lax.all_gather(centered, 'row', axis=0, tiled=True)  147 us
    all_to_all x1, waiting for transfers between devices, on_device(): lax.all_to_all(every_sample, 'col', split_axis=0, concat_axis=1, tiled=True)  127 us
    another operation x5, other arithmetic, on_device(): lax.linalg.triangular_solve(factor, column, left_side=False, lower=True,...  80.9 us
    reduce_sum x8, other arithmetic, broadcast(): return jnp.sum(lax.all_gather(block, axis), axis=0)  33.4 us
    all_gather x1, waiting for transfers between devices, on_device(): own_rows = lax.all_gather(centered, 'col', axis=1, tiled=True)  32.8 us
    all_gather x2, blocking collectives, broadcast(): return jnp.sum(lax.all_gather(block, axis), axis=0)  24.3 us
  transfers between devices with their start and end apart: 9, of which 7 were waited for; matrix products, arithmetic and copies ran while one was open for 30% of the time, Pallas kernels for 0%

profile of v1, /device:TPU:0, one launch (start us, length us, event | category | flops | bytes accessed | tf_op | source)
XLA Modules:
  0.0 1030.9 jit_solution(442244637369376050)
XLA Ops:
  28.7 13.5 %psum.7 = f32[1024]{0:T(1024)S(1)} all-reduce(f32[1024]{0:T(1024)S(1)} %fusion.4), channel_id=1, replica_groups=mesh['row'=4,'col'=8] {'row'}, use_global_device_ids=true, to_apply=%region_2.0 | all-reduce | flops 1024 | bytes 8192 | tf_op jit(solution)/shard_map/psum | solution.py:53
  46.9 147.2 %all-gather.21.cloned.1.call-done = bf16[4096,1024]{0,1:T(8,128)(2,1)} async-done(((bf16[1024,1024]{0,1:T(8,128)(2,1)}), bf16[4096,1024]{0,1:T(8,128)(2,1)}) %all-gather.21.cloned.1.call-update) | async-done | bytes 8388624 | tf_op jit(solution)/shard_map/all_gather | solution.py:58
  194.1 7.9 copy.30
  207.1 126.8 %all-to-all-done = bf16[8,512,1024]{1,2,0:T(8,128)(2,1)} async-done(((bf16[8,512,1024]{1,2,0:T(8,128)(2,1)}), bf16[8,512,1024]{1,2,0:T(8,128)(2,1)}, u32[]{:S(2)}, u32[]{:S(2)}) %all-to-all-start) | async-done | bytes 8388640 | tf_op jit(solution)/shard_map/all_to_all | solution.py:59
  333.8 32.8 %all-gather.19.cloned.1.call-done = bf16[1024,8192]{0,1:T(8,128)(2,1)} async-done(((bf16[1024,1024]{0,1:T(8,128)(2,1)}), bf16[1024,8192]{0,1:T(8,128)(2,1)}) %all-gather.19.cloned.1.call-update) | async-done | bytes 16777232 | tf_op jit(solution)/shard_map/all_gather | solution.py:57
  366.7 15.9 %broadcast_select_fusion.1 = (f32[1024,512]{1,0:T(8,128)}, f32[1024,512]{1,0:T(8,128)S(1)}) fusion(pred[]{:T(512)S(6)} %eq.56, s32[512]{0:T(512)S(1)} %iota_add_fusion.1, s32[1024]{0:T(1024)S(1)} %iota_add_fusion, bf16[1024,8192]{0,1:T(8,128)(2,1)} %all-gather.19.cloned.1.call-done, bf16[512,8192]{0,1:T(8,128)(2,1)} %bitcast.7), kind=kOutput, calls=%fused_computation.118 | convolution fusion | flops 8592031744 | bytes 29366272 | tf_op jit(solution)/shard_map/dot_general | solution.py:60
  385.1 80.4 %all-gather.23.cloned.1.call-done = f32[2048,512]{1,0:T(8,128)} async-done(((f32[512,512]{1,0:T(8,128)}), f32[2048,512]{1,0:T(8,128)}) %all-gather.23.cloned.1.call-update) | async-done | bytes 4194320 | tf_op jit(solution)/shard_map/all_gather | solution.py:13
  470.2 52.1 %all-gather.25.cloned.1.call-done = f32[4096,512]{1,0:T(8,128)} async-done(((f32[512,512]{1,0:T(8,128)}), f32[4096,512]{1,0:T(8,128)}) %all-gather.25.cloned.1.call-update) | async-done | bytes 8388624 | tf_op jit(solution)/shard_map/all_gather | solution.py:13
  530.5 11.7 %cholesky.286 = f32[128,128]{1,0:T(8,128)S(1)} custom-call(f32[128,128]{1,0:T(8,128)S(1)} %cholesky.426), custom_call_target="Cholesky" | custom-call | tf_op jit(solution)/shard_map/jit(cholesky)/cholesky | solution.py:81
  542.4 9.8 custom-call.35
  554.8 12.1 %cholesky.305 = f32[128,128]{1,0:T(8,128)S(1)} custom-call(f32[128,128]{1,0:T(8,128)S(1)} %cholesky.430), custom_call_target="Cholesky" | custom-call | tf_op jit(solution)/shard_map/jit(cholesky)/cholesky | solution.py:81
  566.9 9.8 custom-call.36
  578.3 11.7 %cholesky.326 = f32[128,128]{1,0:T(8,128)S(1)} custom-call(f32[128,128]{1,0:T(8,128)S(1)} %cholesky.435), custom_call_target="Cholesky" | custom-call | tf_op jit(solution)/shard_map/jit(cholesky)/cholesky | solution.py:81
  590.0 9.8 custom-call.37
  601.3 11.9 %cholesky.343 = f32[128,128]{1,0:T(8,128)S(1)} custom-call(f32[128,128]{1,0:T(8,128)S(1)} %convolution_subtract_fusion.17), custom_call_target="Cholesky" | custom-call | tf_op jit(solution)/shard_map/jit(cholesky)/cholesky | solution.py:81
  618.6 11.5 %while.14 = (s32[]{:T(128)}, f32[512,512]{1,0:T(8,128)}, s32[4,2]{0,1:T(2,128)S(1)}, f32[4,128,128]{2,1,0:T(8,128)S(1)}, s32[]{:T(128)}) while((s32[]{:T(128)}, f32[512,512]{1,0:T(8,128)}, s32[4,2]{0,1:T(2,128)S(1)}, f32[4,128,128]{2,1,0:T(8,128)S(1)}, s32[]{:T(128)}) %tuple.86), condition=%wide.while_cond.2, body=%wide.while_body.2.sunk | while | flops 2 | bytes 131181 | solution.py:82
  630.1 39.3 %custom-call.38 = f32[4,128,128]{1,2,0:T(8,128)S(1)} custom-call(f32[4,128,128]{2,1,0:T(8,128)S(1)} %get-tuple-element.72), custom_call_target="InvertDiagBlocksLowerTriangular" | custom-call | tf_op jit(solution)/shard_map/triangular_solve/custom-call.3 | solution.py:82
  674.2 9.4 reduce_sum.94
  702.5 80.9 %all-gather.29.cloned.1.call-done = f32[2048,512]{1,0:T(8,128)} async-done(((f32[512,512]{1,0:T(8,128)}), f32[2048,512]{1,0:T(8,128)}) %all-gather.29.cloned.1.call-update) | async-done | bytes 4194320 | tf_op jit(solution)/shard_map/all_gather | solution.py:13
  788.0 11.9 %all-gather.8 = f32[4,1,512]{2,1,0:T(1,128)S(1)} all-gather(f32[1,1,512]{2,1,0:T(1,128)S(1)} %bitcast.304), channel_id=8, replica_groups=mesh['row'=4,'col'=8] {'row'}, dimensions={0}, use_global_device_ids=true | all-gather | bytes 10240 | tf_op jit(solution)/shard_map/all_gather | solution.py:13
  803.8 12.3 %all-gather.9 = f32[4,1,512]{2,1,0:T(1,128)S(1)} all-gather(f32[1,1,512]{2,1,0:T(1,128)S(1)} %bitcast.305), channel_id=9, replica_groups=mesh['row'=4,'col'=8] {'row'}, dimensions={0}, use_global_device_ids=true | all-gather | bytes 10240 | tf_op jit(solution)/shard_map/all_gather | solution.py:13
  816.2 23.9 %all-gather.31.cloned.1.call-done = f32[4096,512]{1,0:T(8,128)} async-done(((f32[512,512]{1,0:T(8,128)}), f32[4096,512]{1,0:T(8,128)}) %all-gather.31.cloned.1.call-update) | async-done | bytes 8388624 | tf_op jit(solution)/shard_map/all_gather | solution.py:13
  848.4 11.7 %cholesky.358 = f32[128,128]{1,0:T(8,128)S(1)} custom-call(f32[128,128]{1,0:T(8,128)S(1)} %cholesky.439), custom_call_target="Cholesky" | custom-call | tf_op jit(solution)/shard_map/jit(cholesky)/cholesky | solution.py:81
  860.3 9.8 custom-call.40
  872.6 11.8 %cholesky.377 = f32[128,128]{1,0:T(8,128)S(1)} custom-call(f32[128,128]{1,0:T(8,128)S(1)} %cholesky.443), custom_call_target="Cholesky" | custom-call | tf_op jit(solution)/shard_map/jit(cholesky)/cholesky | solution.py:81
  884.5 9.8 custom-call.41
  895.9 11.7 %cholesky.398 = f32[128,128]{1,0:T(8,128)S(1)} custom-call(f32[128,128]{1,0:T(8,128)S(1)} %cholesky.448), custom_call_target="Cholesky" | custom-call | tf_op jit(solution)/shard_map/jit(cholesky)/cholesky | solution.py:81
  907.6 9.8 custom-call.42
  918.9 11.9 %cholesky.415 = f32[128,128]{1,0:T(8,128)S(1)} custom-call(f32[128,128]{1,0:T(8,128)S(1)} %convolution_subtract_fusion.16), custom_call_target="Cholesky" | custom-call | tf_op jit(solution)/shard_map/jit(cholesky)/cholesky | solution.py:81
  937.0 11.7 %while.15 = (s32[]{:T(128)}, f32[512,512]{1,0:T(8,128)}, s32[4,2]{0,1:T(2,128)S(1)}, f32[4,128,128]{2,1,0:T(8,128)S(1)}, s32[]{:T(128)}) while((s32[]{:T(128)}, f32[512,512]{1,0:T(8,128)}, s32[4,2]{0,1:T(2,128)S(1)}, f32[4,128,128]{2,1,0:T(8,128)S(1)}, s32[]{:T(128)}) %tuple.108), condition=%wide.while_cond.2.clone, body=%wide.while_body.2.clone.sunk | while | flops 2 | bytes 131181 | solution.py:82
  948.7 39.3 %custom-call.43 = f32[4,128,128]{1,2,0:T(8,128)S(1)} custom-call(f32[4,128,128]{2,1,0:T(8,128)S(1)} %get-tuple-element.74), custom_call_target="InvertDiagBlocksLowerTriangular" | custom-call | tf_op jit(solution)/shard_map/triangular_solve/custom-call.3 | solution.py:82
  996.9 9.4 reduce_sum.97
  (224 shorter events, 154.1 us)
Async XLA Ops:
  7.2 1.6 copy-start
  7.2 186.9 %all-gather.21.cloned.1.call-start = ((), (), s32[]{:S(2)}) async-start(), calls=%async_computation.2 | async-start | bytes 10485760 | tf_op jit(solution)/shard_map/all_gather | solution.py:58
  8.7 3.5 copy-start.27
  8.7 3.6 copy-start.28
  8.7 3.6 copy-start.29
  19.5 7.6 copy-start.4
  46.1 320.6 %all-gather.19.cloned.1.call-start = ((), (), s32[]{:S(2)}) async-start(), calls=%async_computation.1 | async-start | bytes 18874368 | tf_op jit(solution)/shard_map/all_gather | solution.py:57
  202.0 131.9 %all-to-all-start = ((bf16[8,512,1024]{1,2,0:T(8,128)(2,1)}), bf16[8,512,1024]{1,2,0:T(8,128)(2,1)}, u32[]{:S(2)}, u32[]{:S(2)}) async-start(bf16[8,512,1024]{1,2,0:T(8,128)(2,1)} %bitcast.266), calls=%async_computation | async-start | bytes 16777216 | tf_op jit(solution)/shard_map/all_to_all | solution.py:59
  207.0 258.5 %all-gather.23.cloned.1.call-start = ((), (), s32[]{:S(2)}) async-start(), calls=%async_computation.3 | async-start | bytes 5242880 | tf_op jit(solution)/shard_map/all_gather | solution.py:13
  385.1 137.2 %all-gather.25.cloned.1.call-start = ((), (), s32[]{:S(2)}) async-start(), calls=%async_computation.4 | async-start | bytes 9437184 | tf_op jit(solution)/shard_map/all_gather | solution.py:13
  469.4 204.8 %all-gather.27.cloned.1.call-start = ((), (), s32[]{:S(2)}) async-start(), calls=%async_computation.5 | async-start | bytes 18874368 | tf_op jit(solution)/shard_map/all_gather | solution.py:13
  469.9 313.4 %all-gather.29.cloned.1.call-start = ((), (), s32[]{:S(2)}) async-start(), calls=%async_computation.6 | async-start | bytes 5242880 | tf_op jit(solution)/shard_map/all_gather | solution.py:13
  630.1 41.4 %copy-start.8 = (f32[512,512]{1,0:T(8,128)S(1)}, f32[512,512]{1,0:T(8,128)}, u32[]{:S(2)}) copy-start(f32[512,512]{1,0:T(8,128)} %get-tuple-element.246) | copy-start | bytes 3145732
  669.4 14.2 %copy-start.17 = (f32[4,128,128]{1,2,0:T(8,128)}, f32[4,128,128]{1,2,0:T(8,128)S(1)}, u32[]{:S(2)}) copy-start(f32[4,128,128]{1,2,0:T(8,128)S(1)} %custom-call.38) | copy-start | bytes 786436
  671.5 2.7 copy-start.13
  672.4 1.8 copy-start.20
  683.6 5.4 copy-start.7
  685.5 5.4 copy-start.18
  691.5 8.4 copy-start.12
  691.5 3.6 copy-start.11
  691.5 3.6 copy-start.14
  691.5 3.6 copy-start.21
  691.5 3.6 copy-start.24
  695.1 4.8 copy-start.22
  702.4 137.7 %all-gather.31.cloned.1.call-start = ((), (), s32[]{:S(2)}) async-start(), calls=%async_computation.7 | async-start | bytes 9437184 | tf_op jit(solution)/shard_map/all_gather | solution.py:13
  787.2 12.8 %copy-start.19 = (f32[4,128,128]{1,2,0:T(8,128)S(1)}, f32[4,128,128]{1,2,0:T(8,128)}, u32[]{:S(2)}) copy-start(f32[4,128,128]{1,2,0:T(8,128)} %copy-done.17) | copy-start | bytes 786436
  787.2 209.7 %all-gather.33.cloned.1.call-start = ((), (), s32[]{:S(2)}) async-start(), calls=%async_computation.8 | async-start | bytes 18874368 | tf_op jit(solution)/shard_map/all_gather | solution.py:13
  948.7 45.6 %copy-start.9 = (f32[512,512]{1,0:T(8,128)S(1)}, f32[512,512]{1,0:T(8,128)}, u32[]{:S(2)}) copy-start(f32[512,512]{1,0:T(8,128)} %get-tuple-element.247) | copy-start | bytes 3145732
  1006.3 4.5 copy-start.6
  1016.3 1.8 copy-start.3
  1016.3 1.8 copy-start.23
  1018.1 5.5 copy-start.1
  (7 other events, 7.5 us)
Sparse Core Ops, SparseCore 0:
  46.2 147.8 all-gather.20
  196.0 170.6 all-gather.18
  385.2 80.2 all-gather.22
  469.5 52.7 all-gather.24
  524.6 89.8 all-gather.26
  702.5 80.7 all-gather.28
  787.3 52.7 all-gather.30
  842.6 89.7 all-gather.32
